TPU v7x, 512 devices: a whole 4x4x16 slice. The times are simulated.
512 devices in a mesh: rows: 64 (over x, z), cols: 8 (over y, core).
Axes of the slice: x: 4, y: 4, z: 16, core: 2. Of those that a mesh axis runs over, the one named last changes fastest.
Arguments:
- sketch: bfloat16 [131072, 256], P(('rows', 'cols')), may hold values from -6 to 6
- blocks: bfloat16 [4096, 256, 256], P(('rows', 'cols')), may hold values from -0.375 to 0.375
- block_rows: int32 [4096], P(('rows', 'cols')), may hold values from 0 to 3, as said below
- block_cols: int32 [4096], P(('rows', 'cols')), may hold values from 0 to 63
- counts: int32 [512], P(('rows', 'cols')), may hold values from 1 to 8, as said below
Outputs:
- basis: float32 [65536, 256], P(('rows', 'cols'))
- factor: float32 [256, 256], replicated
Inputs may be any that keep to these rules, and one draw needn't show every extreme that they name: Within one device's 8 slots the pairs (block_rows, block_cols) are distinct. `counts`: some device has exactly 8 live slots.
All inputs are finite; a program needn't handle non-finite values.
Results may differ from a plain program's by a relative error of at most 0.0003.
Values may be sent and summed in bfloat16 or wider, within the bound.
A program may use at most 64 MiB of HBM per device.

v0:
```python
import jax
import jax.numpy as jnp
from jax import lax
from jax.sharding import PartitionSpec as P

RB = 4


def local(sketch, blocks, block_rows, block_cols, counts):
    highest = lax.Precision.HIGHEST
    slots, width, _ = blocks.shape
    columns = sketch.shape[1]
    live_count = counts[0]
    starts = block_cols * width
    panel = lax.all_gather(sketch, "rows", axis=0, tiled=True)
    chosen = jax.vmap(lambda offset: lax.dynamic_slice_in_dim(panel, offset, width, 0))(starts)
    products = jnp.einsum("bij,bjk->bik", blocks, chosen, preferred_element_type=jnp.float32)
    selector = (
        (block_rows[:, None] == jnp.arange(RB, dtype=jnp.int32)[None, :])
        & (jnp.arange(slots, dtype=jnp.int32) < live_count)[:, None]
    ).astype(jnp.float32)
    partial_rows = jnp.einsum("br,bik->rik", selector, products, precision=highest)
    partial_rows = partial_rows.reshape(RB * width, columns)
    total_rows = RB * width * lax.axis_size("rows")
    slab_total = lax.psum(partial_rows, "cols")
    gram_matrix = lax.psum(jnp.dot(slab_total.T, slab_total, precision=highest), "rows")
    share_rows = slab_total.shape[0] // lax.axis_size("cols")
    own_rows = lax.dynamic_slice_in_dim(
        slab_total, lax.axis_index("cols") * share_rows, share_rows, 0
    )
    lower_factor = jnp.linalg.cholesky(gram_matrix)
    root_rows = jnp.sqrt(jnp.float32(total_rows))
    solved = lax.linalg.triangular_solve(
        lower_factor, own_rows, left_side=False, lower=True, transpose_a=True
    )
    return (solved * root_rows, lower_factor.T / root_rows)


def solution(mesh):
    in_specs = (
        P(("rows", "cols"), None),
        P(("rows", "cols"), None, None),
        P(("rows", "cols")),
        P(("rows", "cols")),
        P(("rows", "cols")),
    )
    out_specs = (P(("rows", "cols"), None), P())
    return jax.shard_map(local, mesh=mesh, in_specs=in_specs, out_specs=out_specs, check_vma=False)
```

profile of v0, /device:TPU:8, one launch (start us, length us, event | category | flops | bytes accessed | tf_op | source)
XLA Modules:
  0.0 611.1 jit_solution(694707326038857665)
XLA Ops:
  7.2 0.0 copy-start
  7.2 0.0 all-gather.2.cloned.1.call-start
  7.2 0.7 all-gather.2.cloned.1.call-update
  7.9 0.0 all-reduce.5.cloned.1.call-start
  8.0 0.7 fusion.16
  9.3 162.0 %all-gather.2.cloned.1.call-done = bf16[16384,256]{1,0:T(8,128)(2,1)} async-done(((bf16[256,256]{1,0:T(8,128)(2,1)}), bf16[16384,256]{1,0:T(8,128)(2,1)}) %all-gather.2.cloned.1.call-update) | async-done | bytes 8388624 | tf_op jit(solution)/shard_map/all_gather | solution.py:15
  171.3 17.0 %while.2 = (s32[]{:T(128)}, bf16[16384,256]{1,0:T(8,128)(2,1)}, s32[8,2]{0,1:T(2,128)S(1)}, bf16[8,256,256]{2,1,0:T(8,128)(2,1)S(1)}, s32[]{:T(128)}) while((s32[]{:T(128)}, bf16[16384,256]{1,0:T(8,128)(2,1)}, s32[8,2]{0,1:T(2,128)S(1)}, bf16[8,256,256]{2,1,0:T(8,128)(2,1)S(1)}, s32[]{:T(128)}) %tuple.41), condition=%wide.while_cond, body=%wide.while_body.sunk | while | flops 2 | bytes 262241 | solution.py:16
  171.3 0.1 constant_dynamic-slice_fusion.4
  171.4 0.5 slice.69
  171.9 1.5 bitcast_dynamic-update-slice_fusion.4
  173.4 0.1 constant_dynamic-slice_fusion.4
  173.5 0.5 slice.69
  174.0 1.5 bitcast_dynamic-update-slice_fusion.4
  175.6 0.1 constant_dynamic-slice_fusion.4
  175.7 0.5 slice.69
  176.2 1.5 bitcast_dynamic-update-slice_fusion.4
  177.7 0.1 constant_dynamic-slice_fusion.4
  177.8 0.5 slice.69
  178.3 1.5 bitcast_dynamic-update-slice_fusion.4
  179.8 0.1 constant_dynamic-slice_fusion.4
  179.9 0.5 slice.69
  180.4 1.5 bitcast_dynamic-update-slice_fusion.4
  182.0 0.1 constant_dynamic-slice_fusion.4
  182.0 0.5 slice.69
  182.6 1.5 bitcast_dynamic-update-slice_fusion.4
  184.1 0.1 constant_dynamic-slice_fusion.4
  184.2 0.5 slice.69
  184.7 1.5 bitcast_dynamic-update-slice_fusion.4
  186.2 0.1 constant_dynamic-slice_fusion.4
  186.3 0.5 slice.69
  186.8 1.5 bitcast_dynamic-update-slice_fusion.4
  188.4 0.0 copy-done
  188.4 1.8 fusion.19
  190.2 0.0 copy-start.1
  190.2 2.2 copy.16
  192.4 0.0 copy-done.1
  192.4 1.1 fusion
  193.5 1.2 copy.11
  194.7 0.0 all-reduce.5.cloned.1.call-update
  194.8 0.2 all-reduce.7.cloned.1.call-start
  195.0 70.9 %all-reduce.5.cloned.1.call-done = f32[1024,256]{1,0:T(8,128)} async-done(((f32[1024,256]{1,0:T(8,128)}), f32[1024,256]{1,0:T(8,128)}) %all-reduce.5.cloned.1.call-update) | async-done | bytes 1048592 | tf_op jit(solution)/shard_map/psum | solution.py:25
  265.9 4.1 fusion.20
  269.9 0.0 all-reduce.7.cloned.1.call-update
  270.0 268.6 %all-reduce.7.cloned.1.call-done = f32[256,256]{0,1:T(8,128)} async-done(((f32[256,256]{0,1:T(8,128)}), f32[256,256]{0,1:T(8,128)}) %all-reduce.7.cloned.1.call-update) | async-done | bytes 262160 | tf_op jit(solution)/shard_map/psum | solution.py:26
  538.6 1.1 copy.13
  539.6 1.0 fusion.2
  540.6 11.7 %cholesky.50 = f32[128,128]{1,0:T(8,128)S(1)} custom-call(f32[128,128]{1,0:T(8,128)S(1)} %cholesky.118), custom_call_target="Cholesky" | custom-call | tf_op jit(solution)/shard_map/jit(cholesky)/cholesky | solution.py:31
  552.4 9.8 %custom-call.14 = f32[1,128,128]{1,2,0:T(8,128)S(1)} custom-call(f32[1,128,128]{2,1,0:T(8,128)S(1)} %get-tuple-element.45), custom_call_target="InvertDiagBlocksLowerTriangular" | custom-call | tf_op jit(solution)/shard_map/jit(cholesky)/cholesky | solution.py:31
  562.2 0.2 constant_dynamic-update-slice_fusion.1
  562.5 0.3 convolution_subtract_fusion.1
  562.7 11.7 %cholesky.105 = f32[128,128]{1,0:T(8,128)S(1)} custom-call(f32[128,128]{1,0:T(8,128)S(1)} %convolution_subtract_fusion.1), custom_call_target="Cholesky" | custom-call | tf_op jit(solution)/shard_map/jit(cholesky)/cholesky | solution.py:31
  574.5 0.8 compare_reduce_fusion
  576.6 0.1 triangular_solve.58
  576.7 4.0 while.3
  576.7 0.6 fusion.30
  577.3 1.4 bitcast_dynamic-update-slice_fusion.5
  578.7 0.6 fusion.30
  579.3 1.4 bitcast_dynamic-update-slice_fusion.5
  580.7 19.7 %custom-call.15 = f32[2,128,128]{1,2,0:T(8,128)S(1)} custom-call(f32[2,128,128]{2,1,0:T(8,128)S(1)} %get-tuple-element.17), custom_call_target="InvertDiagBlocksLowerTriangular" | custom-call | tf_op jit(solution)/shard_map/triangular_solve | solution.py:33
  600.4 1.1 fusion.6
  601.5 1.1 convolution_subtract_fusion
  602.7 0.3 fusion.4
  603.0 0.8 copy.14
  603.7 0.8 copy.15
  (13 shorter events, 0.2 us)
Async XLA Ops:
  7.2 181.2 %copy-start = (bf16[8,256,256]{2,1,0:T(8,128)(2,1)S(1)}, bf16[8,256,256]{2,1,0:T(8,128)(2,1)}, u32[]{:S(2)}) copy-start(bf16[8,256,256]{2,1,0:T(8,128)(2,1)} %param.6) | copy-start | bytes 3145732
  7.2 164.1 %all-gather.2.cloned.1.call-start = ((), (), s32[]{:S(2)}) async-start(), calls=%async_computation | async-start | bytes 8519680 | tf_op jit(solution)/shard_map/all_gather | solution.py:15
  7.9 258.0 %all-reduce.5.cloned.1.call-start = ((), (), s32[]{:S(2)}) async-start(), calls=%async_computation.1 | async-start | bytes 2097152 | tf_op jit(solution)/shard_map/psum | solution.py:25
  190.2 2.2 copy-start.1
  194.8 343.8 %all-reduce.7.cloned.1.call-start = ((), (), s32[]{:S(2)}) async-start(), calls=%async_computation.2 | async-start | bytes 524288 | tf_op jit(solution)/shard_map/psum | solution.py:26
Sparse Core Ops, SparseCore 0:
  10.9 160.3 all-gather.1
  194.9 70.9 all-reduce.4
  270.1 268.4 all-reduce.6
where the time goes:
time: 612 us; the launch traced here: 611 us
  waiting for transfers between devices  502 us (82%)
  other arithmetic  55.5 us (9%)
  local copies, waits for them, and re-layouts  27 us (4%)
  between operations  15.9 us (3%)
  matrix products  10 us (2%)
    psum x1, waiting for transfers between devices, local(): lax.psum(jnp.dot(slab_total.T, slab_total, precision=highest), 'rows')  269 us
    all_gather x1, waiting for transfers between devices, local(): panel = lax.all_gather(sketch, 'rows', axis=0, tiled=True)  162 us
    psum x1, waiting for transfers between devices, local(): slab_total = lax.psum(partial_rows, 'cols')  70.9 us
    another operation x6, other arithmetic, local(): lower_factor = jnp.linalg.cholesky(gram_matrix)  34.2 us
    another operation x2, other arithmetic, local(): lax.linalg.triangular_solve(lower_factor, own_rows, left_side=False, lowe...  19.7 us
    gather x24, local copies, waits for them, and re-layouts  16.9 us
  transfers between devices with their start and end apart: 3, of which 3 were waited for; matrix products, arithmetic and copies ran while one was open for 0% of the time, Pallas kernels for 0%

commit v1 on v0

--- a/solution.py
+++ b/solution.py
@@ -4,6 +4,14 @@
 from jax.sharding import PartitionSpec as P
 
 RB = 4
+
+
+def map_the_paths(payload, mesh_ax):
+    degree = lax.axis_size(mesh_ax)
+    u_next = payload
+    for nth in [[(at, at ^ no) for at in range(degree)] for no in (1, 2, 4, 8, 16) if no < degree]:
+        u_next = u_next + lax.ppermute(u_next, perm=nth, axis_name=mesh_ax)
+    return u_next
 
 
 def local(sketch, blocks, block_rows, block_cols, counts):
@@ -22,7 +30,7 @@
     partial_rows = jnp.einsum("br,bik->rik", selector, products, precision=highest)
     partial_rows = partial_rows.reshape(RB * width, columns)
     total_rows = RB * width * lax.axis_size("rows")
-    slab_total = lax.psum(partial_rows, "cols")
+    slab_total = map_the_paths(partial_rows, "cols")
     gram_matrix = lax.psum(jnp.dot(slab_total.T, slab_total, precision=highest), "rows")
     share_rows = slab_total.shape[0] // lax.axis_size("cols")
     own_rows = lax.dynamic_slice_in_dim(

time: 612 us -> 591 us (0.966)
  waiting for transfers between devices: 502 us -> 475 us
  starting transfers between devices: 0.3 us -> 8.83 us
    psum x1 -> x0, waiting for transfers between devices: 70.9 us -> none  [local(): slab_total = lax.psum(partial_rows, 'cols')]
    ppermute x0 -> x3, waiting for transfers between devices: none -> 50.6 us  [map_the_paths(): u_next = u_next + lax.ppermute(u_next, perm=nth, axis_name=mesh_ax)]
    ppermute x0 -> x3, starting transfers between devices: none -> 8.76 us  [map_the_paths(): u_next = u_next + lax.ppermute(u_next, perm=nth, axis_name=mesh_ax)]
    psum x1, waiting for transfers between devices: 269 us -> 262 us  [local(): lax.psum(jnp.dot(slab_total.T, slab_total, precision=highest), 'rows')]
  transfers between devices with their start and end apart: 3 -> 5, of which waited for: 3 -> 5; matrix products, arithmetic and copies ran while one was open for 0% -> 0% of each run, Pallas kernels for 0% -> 0%
where the time goes in v1:
time: 591 us; the launch traced here: 590 us
  waiting for transfers between devices  475 us (80%)
  other arithmetic  55.9 us (9%)
  local copies, waits for them, and re-layouts  27.3 us (5%)
  between operations  16.2 us (3%)
  starting transfers between devices  8.83 us (1%)
  matrix products  6.76 us (1%)
    psum x1, waiting for transfers between devices, local(): lax.psum(jnp.dot(slab_total.T, slab_total, precision=highest), 'rows')  262 us
    all_gather x1, waiting for transfers between devices, local(): panel = lax.all_gather(sketch, 'rows', axis=0, tiled=True)  162 us
    ppermute x3, waiting for transfers between devices, map_the_paths(): u_next = u_next + lax.ppermute(u_next, perm=nth, axis_name=mesh_ax)  50.6 us
    another operation x6, other arithmetic, local(): lower_factor = jnp.linalg.cholesky(gram_matrix)  34.1 us
    another operation x2, other arithmetic, local(): lax.linalg.triangular_solve(lower_factor, own_rows, left_side=False, lowe...  19.7 us
    gather x24, local copies, waits for them, and re-layouts  18.2 us
  transfers between devices with their start and end apart: 5, of which 5 were waited for; matrix products, arithmetic and copies ran while one was open for 0% of the time, Pallas kernels for 0%

profile of v1, /device:TPU:8, one launch (start us, length us, event | category | flops | bytes accessed | tf_op | source)
XLA Modules:
  0.0 590.0 jit_solution(13805066172462341186)
XLA Ops:
  7.2 0.7 all-gather.2.cloned.1.call-update
  7.9 0.0 all-reduce.4.cloned.1.call-start
  8.0 0.7 fusion.17
  9.3 162.0 %all-gather.2.cloned.1.call-done = bf16[16384,256]{1,0:T(8,128)(2,1)} async-done(((bf16[256,256]{1,0:T(8,128)(2,1)}), bf16[16384,256]{1,0:T(8,128)(2,1)}) %all-gather.2.cloned.1.call-update) | async-done | bytes 8388624 | tf_op jit(solution)/shard_map/all_gather | solution.py:23
  171.3 18.3 %while.2 = (s32[]{:T(128)}, bf16[16384,256]{1,0:T(8,128)(2,1)}, s32[8,2]{0,1:T(2,128)S(1)}, bf16[8,256,256]{2,1,0:T(8,128)(2,1)S(1)}, s32[]{:T(128)}) while((s32[]{:T(128)}, bf16[16384,256]{1,0:T(8,128)(2,1)}, s32[8,2]{0,1:T(2,128)S(1)}, bf16[8,256,256]{2,1,0:T(8,128)(2,1)S(1)}, s32[]{:T(128)}) %tuple.41), condition=%wide.while_cond, body=%wide.while_body.sunk | while | flops 2 | bytes 262241 | solution.py:24
  171.3 0.1 constant_dynamic-slice_fusion.4
  171.4 0.6 slice.69
  172.0 1.6 bitcast_dynamic-update-slice_fusion.4
  173.6 0.1 constant_dynamic-slice_fusion.4
  173.7 0.6 slice.69
  174.3 1.6 bitcast_dynamic-update-slice_fusion.4
  175.9 0.1 constant_dynamic-slice_fusion.4
  176.0 0.6 slice.69
  176.6 1.6 bitcast_dynamic-update-slice_fusion.4
  178.2 0.1 constant_dynamic-slice_fusion.4
  178.3 0.6 slice.69
  178.8 1.6 bitcast_dynamic-update-slice_fusion.4
  180.5 0.1 constant_dynamic-slice_fusion.4
  180.6 0.6 slice.69
  181.1 1.6 bitcast_dynamic-update-slice_fusion.4
  182.8 0.1 constant_dynamic-slice_fusion.4
  182.9 0.6 slice.69
  183.4 1.6 bitcast_dynamic-update-slice_fusion.4
  185.1 0.1 constant_dynamic-slice_fusion.4
  185.2 0.6 slice.69
  185.7 1.6 bitcast_dynamic-update-slice_fusion.4
  187.4 0.1 constant_dynamic-slice_fusion.4
  187.4 0.6 slice.69
  188.0 1.6 bitcast_dynamic-update-slice_fusion.4
  189.7 1.8 fusion.20
  191.5 2.2 copy.16
  193.7 1.1 fusion
  194.8 0.2 copy.11
  195.0 1.9 collective-permute-start
  197.0 2.6 collective-permute-done
  199.6 0.1 bitcast_add_fusion.1
  199.7 2.5 collective-permute-start.1
  202.2 24.6 %collective-permute-done.1 = f32[1024,256]{1,0:T(8,128)S(1)} collective-permute-done((f32[1024,256]{1,0:T(8,128)S(1)}, f32[1024,256]{1,0:T(8,128)S(1)}, u32[]{:S(2)}, u32[]{:S(2)}) %collective-permute-start.1) | collective-permute-done | bytes 1048608 | tf_op jit(solution)/shard_map/ppermute | solution.py:13
  226.8 0.1 add.43
  227.0 4.3 collective-permute-start.2
  231.3 23.4 %collective-permute-done.2 = f32[1024,256]{1,0:T(8,128)S(1)} collective-permute-done((f32[1024,256]{1,0:T(8,128)S(1)}, f32[1024,256]{1,0:T(8,128)S(1)}, u32[]{:S(2)}, u32[]{:S(2)}) %collective-permute-start.2) | collective-permute-done | bytes 1048608 | tf_op jit(solution)/shard_map/ppermute | solution.py:13
  254.7 0.1 add.44
  254.8 2.5 fusion.21
  257.4 261.5 %all-reduce.4.cloned.1.call-done = f32[256,256]{0,1:T(8,128)} async-done(((f32[256,256]{0,1:T(8,128)}), f32[256,256]{0,1:T(8,128)}) %all-reduce.4.cloned.1.call-update) | async-done | bytes 262160 | tf_op jit(solution)/shard_map/psum | solution.py:34
  518.9 1.1 copy.13
  520.0 1.0 fusion.2
  521.0 11.7 %cholesky.50 = f32[128,128]{1,0:T(8,128)S(1)} custom-call(f32[128,128]{1,0:T(8,128)S(1)} %cholesky.118), custom_call_target="Cholesky" | custom-call | tf_op jit(solution)/shard_map/jit(cholesky)/cholesky | solution.py:39
  532.8 9.8 %custom-call.14 = f32[1,128,128]{1,2,0:T(8,128)S(1)} custom-call(f32[1,128,128]{2,1,0:T(8,128)S(1)} %get-tuple-element.45), custom_call_target="InvertDiagBlocksLowerTriangular" | custom-call | tf_op jit(solution)/shard_map/jit(cholesky)/cholesky | solution.py:39
  542.6 0.2 constant_dynamic-update-slice_fusion.1
  542.8 0.3 convolution_subtract_fusion
  543.1 11.8 %cholesky.105 = f32[128,128]{1,0:T(8,128)S(1)} custom-call(f32[128,128]{1,0:T(8,128)S(1)} %convolution_subtract_fusion), custom_call_target="Cholesky" | custom-call | tf_op jit(solution)/shard_map/jit(cholesky)/cholesky | solution.py:39
  555.0 0.7 compare_reduce_fusion
  557.0 0.1 triangular_solve.58
  557.0 3.9 while.3
  557.0 0.6 fusion.30
  557.6 1.4 bitcast_dynamic-update-slice_fusion.5
  559.0 0.6 fusion.30
  559.6 1.4 bitcast_dynamic-update-slice_fusion.5
  561.0 19.7 %custom-call.15 = f32[2,128,128]{1,2,0:T(8,128)S(1)} custom-call(f32[2,128,128]{2,1,0:T(8,128)S(1)} %get-tuple-element.17), custom_call_target="InvertDiagBlocksLowerTriangular" | custom-call | tf_op jit(solution)/shard_map/triangular_solve | solution.py:41
  580.7 0.3 fusion.7
  581.0 0.3 fusion.5
  581.2 0.3 fusion.4
  581.6 0.8 copy.14
  582.3 0.8 copy.15
  (19 shorter events, 0.2 us)
Async XLA Ops:
  7.2 182.5 %copy-start = (bf16[8,256,256]{2,1,0:T(8,128)(2,1)S(1)}, bf16[8,256,256]{2,1,0:T(8,128)(2,1)}, u32[]{:S(2)}) copy-start(bf16[8,256,256]{2,1,0:T(8,128)(2,1)} %param.6) | copy-start | bytes 3145732
  7.2 164.1 %all-gather.2.cloned.1.call-start = ((), (), s32[]{:S(2)}) async-start(), calls=%async_computation | async-start | bytes 8519680 | tf_op jit(solution)/shard_map/all_gather | solution.py:23
  7.9 511.0 %all-reduce.4.cloned.1.call-start = ((), (), s32[]{:S(2)}) async-start(), calls=%async_computation.1 | async-start | bytes 524288 | tf_op jit(solution)/shard_map/psum | solution.py:34
  191.5 2.2 copy-start.1
  195.0 4.6 collective-permute-start
  199.7 27.1 %collective-permute-start.1 = (f32[1024,256]{1,0:T(8,128)S(1)}, f32[1024,256]{1,0:T(8,128)S(1)}, u32[]{:S(2)}, u32[]{:S(2)}) collective-permute-start(f32[1024,256]{1,0:T(8,128)S(1)} %bitcast_add_fusion.1), channel_id=1, source_target_pairs={{0,2},{1,3},{2,0},{3,1},{4,6},{5,7},{6,4},{7,5},{8,10},{9,11},{10,... | collective-permute-start | bytes 3145736 | tf_op jit(solution)/shard_map/ppermute | solution.py:13
  227.0 27.7 %collective-permute-start.2 = (f32[1024,256]{1,0:T(8,128)S(1)}, f32[1024,256]{1,0:T(8,128)S(1)}, u32[]{:S(2)}, u32[]{:S(2)}) collective-permute-start(f32[1024,256]{1,0:T(8,128)S(1)} %add.43), channel_id=1, source_target_pairs={{0,4},{1,5},{2,6},{3,7},{4,0},{5,1},{6,2},{7,3},{8,12},{9,13},{10,... | collective-permute-start | bytes 3145736 | tf_op jit(solution)/shard_map/ppermute | solution.py:13
Sparse Core Ops, SparseCore 0:
  10.9 160.3 all-gather.1
  257.5 261.3 all-reduce.3
